TPU v7x, 256 devices: a whole 4x4x8 slice. The times are simulated.
256 devices in a mesh: seq: 32 (over z, y), grp: 8 (over x, core).
Axes of the slice: x: 4, y: 4, z: 8, core: 2. Of those that a mesh axis runs over, the one named last changes fastest.
Arguments:
- x_in: bfloat16 [4096, 8192], P('seq', 'grp'), may hold values from -6 to 6
- multiplier_channels: bfloat16 [4096, 8192], P('seq', 'grp'), may hold values from -6 to 6
- b_proj: bfloat16 [4096, 1024], P('seq', 'grp'), may hold values from -6 to 6
- c_proj: bfloat16 [4096, 1024], P('seq', 'grp'), may hold values from -0.5 to 0.5
- dt_raw: float32 [4096, 64], P('seq', 'grp'), as said below
- dt_bias: float32 [64], P('grp'), may hold values from -3.5 to -1.5
- a_log: float32 [64], P('grp'), as said below
- skip_d: float32 [64], P('grp'), may hold values from 0.2 to 1
- norm_gain: float32 [8192], P('grp'), may hold values from 0.5 to 1.5
- w_out: bfloat16 [8192, 8192], P('grp', 'seq'), may hold values from -0.03125 to 0.03125
Outputs:
- mixed: bfloat16 [4096, 8192], P('seq', 'grp')
Inputs may be any that keep to these rules, and one draw needn't show every extreme that they name: `dt_raw`: step size offsets, with bursts at a few positions of the sequence shared by all heads. `a_log`: log decay rates per head, between log(0.1 / (0.08 * 4096)) and log(0.6).
All inputs are finite; a program needn't handle non-finite values.
Results may differ from a plain program's by a relative error of at most 0.0049.
Values may be sent and summed in bfloat16 or wider, within the bound.
A program may use at most 128 MiB of HBM per device.

v0:
```python
import math
import jax
import jax.numpy as jnp
from jax import lax
from jax.sharding import PartitionSpec as P

CHANNEL_WIDTH = 128
STATE = 128
HIGH = lax.Precision.HIGHEST


def prefix(array, axis, combine, identity):
    length, mine = (lax.axis_size(axis), lax.axis_index(axis))
    everything = jax.tree.map(lambda part: lax.all_gather(part, axis), array)
    start = jax.tree.map(
        lambda part, zero: jnp.broadcast_to(jnp.asarray(zero, part.dtype), part.shape),
        array,
        identity,
    )

    def turn(k, before):
        reached = k < mine
        new = combine(before, jax.tree.map(lambda part: part[k], everything))
        return jax.tree.map(lambda a, b: jnp.where(reached, a, b), new, before)

    return lax.fori_loop(0, length, turn, start)


def ssd_blocks(xf, dt, la, bm, cm, braw, craw, init):
    length, heads, width = xf.shape
    groups = bm.shape[1]
    ratio = heads // groups
    block = math.gcd(length, 256)
    count = length // block

    def step(state, blk):
        xb, dtb, lab, bb, cb, bnar, cnar = blk
        cum = jnp.cumsum(lab, axis=0)
        attention_logits = jnp.einsum(
            "tgn,sgn->gts", cnar, bnar, preferred_element_type=jnp.float32
        )
        attention_logits = jnp.repeat(attention_logits, ratio, axis=0)
        diff = cum.T[:, :, None] - cum.T[:, None, :]
        rows = lax.broadcasted_iota(jnp.int32, (block, block), 0)
        cols = lax.broadcasted_iota(jnp.int32, (block, block), 1)
        mask = (rows >= cols)[None, :, :]
        decay = jnp.exp(jnp.where(mask, diff, -1e30))
        mixing = decay * attention_logits * dtb.T[:, None, :]
        outs = jnp.einsum("hts,shp->thp", mixing, xb, precision=HIGH)
        cheads = jnp.repeat(cb, ratio, axis=1)
        incoming_channel_bundles = jnp.repeat(bb, ratio, axis=1)
        outs = outs + jnp.exp(cum)[:, :, None] * jnp.einsum(
            "thn,hpn->thp", cheads, state, precision=HIGH
        )
        weights = jnp.exp(cum[-1][None, :] - cum) * dtb
        fresh = jnp.einsum("sh,shp,shn->hpn", weights, xb, incoming_channel_bundles, precision=HIGH)
        state = jnp.exp(cum[-1])[:, None, None] * state + fresh
        return (state, outs)

    blocks = (
        xf.reshape(count, block, heads, width),
        dt.reshape(count, block, heads),
        la.reshape(count, block, heads),
        bm.reshape(count, block, groups, -1),
        cm.reshape(count, block, groups, -1),
        braw.reshape(count, block, groups, -1),
        craw.reshape(count, block, groups, -1),
    )
    final, outs = lax.scan(step, init, blocks)
    return (outs.reshape(length, heads, width), final, jnp.sum(la, axis=0))


def gated_norm_output(y, multiplier_channels, norm_gain, groups):
    length = y.shape[0]
    gated = y.reshape(length, -1) * jax.nn.silu(multiplier_channels.astype(jnp.float32))
    split = gated.reshape(length, groups, -1)
    split = split * lax.rsqrt(jnp.mean(split * split, axis=-1, keepdims=True) + 1e-05)
    return (split.reshape(length, -1) * norm_gain).astype(jnp.bfloat16)


def combine_states(earlier_state, later):
    return (earlier_state[0] * later[0], later[0][:, None, None] * earlier_state[1] + later[1])


def shards(
    x_in, multiplier_channels, b_proj, c_proj, dt_raw, dt_bias, a_log, skip_d, norm_gain, w_out
):
    length = x_in.shape[0]
    heads = dt_raw.shape[1]
    groups = b_proj.shape[1] // STATE
    xf = x_in.astype(jnp.float32).reshape(length, heads, CHANNEL_WIDTH)
    dt = jax.nn.softplus(dt_raw + dt_bias)
    la = -jnp.exp(a_log) * dt
    braw = b_proj.reshape(length, groups, STATE)
    craw = c_proj.reshape(length, groups, STATE)
    bm = braw.astype(jnp.float32)
    cm = craw.astype(jnp.float32)
    empty = jnp.zeros((heads, CHANNEL_WIDTH, STATE), jnp.float32)
    y, local_end, total = ssd_blocks(xf, dt, la, bm, cm, braw, craw, empty)
    identity = (jnp.ones((heads,), jnp.float32), empty)
    carried = prefix((jnp.exp(total), local_end), "seq", combine_states, identity)
    cum = jnp.cumsum(la, axis=0)
    cheads = jnp.repeat(cm, heads // groups, axis=1)
    y = y + jnp.exp(cum)[:, :, None] * jnp.einsum(
        "thn,hpn->thp", cheads, carried[1], precision=HIGH
    )
    y = y + skip_d[None, :, None] * xf
    normed = gated_norm_output(y, multiplier_channels, norm_gain, groups)
    partial_out = jnp.dot(
        normed, lax.all_gather(w_out, "seq", axis=1, tiled=True), preferred_element_type=jnp.float32
    )
    return lax.psum_scatter(partial_out, "grp", scatter_dimension=1, tiled=True).astype(
        jnp.bfloat16
    )


def solution(mesh):
    return jax.shard_map(
        shards,
        mesh=mesh,
        in_specs=(
            P("seq", "grp"),
            P("seq", "grp"),
            P("seq", "grp"),
            P("seq", "grp"),
            P("seq", "grp"),
            P("grp"),
            P("grp"),
            P("grp"),
            P("grp"),
            P("grp", "seq"),
        ),
        out_specs=P("seq", "grp"),
        check_vma=False,
    )
```

profile of v0, /device:TPU:8, one launch (start us, length us, event | category | flops | bytes accessed | tf_op | source)
XLA Modules:
  0.0 363.0 jit_solution(16501429066232339684)
XLA Ops:
  11.2 1.4 convolution_add_fusion
  14.4 1.3 dynamic-slice.6
  16.4 74.4 %all-reduce = f32[256]{0:T(256)S(1)} all-reduce(f32[256]{0:T(256)S(1)} %exponential_dynamic-update-slice_fusion), channel_id=2, replica_groups=mesh['seq'=32,'grp'=8] {'seq'}, use_global_device_ids=true, to_apply=%add | all-reduce | flops 256 | bytes 2048
  92.6 1.2 fusion.5
  93.8 61.4 %all-gather.7.cloned.1.call-done = f32[256,128,128]{2,1,0:T(8,128)} async-done(((f32[8,128,128]{2,1,0:T(8,128)}), f32[256,128,128]{2,1,0:T(8,128)}) %all-gather.7.cloned.1.call-update) | async-done | bytes 16777232 | tf_op jit(solution)/shard_map/all_gather | solution.py:14
  155.2 39.0 %while.9 = (s32[]{:T(128)}, f32[8,128,128]{2,1,0:T(8,128)S(1)}, s32[]{:T(128)}, f32[32,8]{1,0:T(8,128)S(1)}, f32[32,8,128,128]{3,2,1,0:T(8,128)}, /*index=5*/s32[]{:T(128)}, s32[]{:T(128)}) while((s32[]{:T(128)}, f32[8,128,128]{2,1,0:T(8,128)S(1)}, s32[]{:T(128)}, f32[32,8]{1,0:T(8,128)S(1)}, f32[32,8,128,128]{3,2,1,0:T(8,128)}, ...), condition=%wide.region_3.4_spmd.clone, body=%wide.region_2.3_spmd.clone.sunk | while | flops 524292 | bytes 1573065 | solution.py:26
  156.4 1.2 fusion.41
  157.6 1.2 fusion.41
  161.3 1.2 fusion.41
  162.5 1.2 fusion.41
  166.1 1.2 fusion.41
  167.3 1.2 fusion.41
  168.6 1.2 fusion.41
  169.8 1.2 fusion.41
  171.1 1.2 fusion.41
  173.5 1.2 fusion.41
  174.7 1.2 fusion.41
  175.9 1.2 fusion.41
  177.2 1.2 fusion.41
  178.4 1.2 fusion.41
  179.6 1.2 fusion.41
  180.8 1.2 fusion.41
  183.2 1.2 fusion.41
  186.9 1.2 fusion.41
  188.1 1.2 fusion.41
  191.8 1.2 fusion.41
  193.0 1.2 fusion.41
  194.2 1.9 fusion.3
  196.5 108.9 %all-gather.5.cloned.1.call-done = bf16[1024,8192]{1,0:T(8,128)(2,1)} async-done(((bf16[1024,256]{1,0:T(8,128)(2,1)}), bf16[1024,8192]{1,0:T(8,128)(2,1)}) %all-gather.5.cloned.1.call-update) | async-done | bytes 16777232 | tf_op jit(solution)/shard_map/all_gather | solution.py:110
  305.4 10.2 %fusion.15 = f32[128,8192]{1,0:T(8,128)} fusion(bf16[1024,8192]{1,0:T(8,128)(2,1)} %all-gather.5.cloned.1.call-done, f32[1024]{0:T(1024)S(1)} %copy-done.1, f32[128]{0:T(128)S(1)} %add_rsqrt_fusion, f32[128,1024]{1,0:T(8,128)S(1)} %copy.41, bf16[128,1024]{1,0:T(8,128)(2,1)S(1)} %copy-done), kind=kOutput, calls=%fused_computation.27 | convolution fusion | flops 2148663296 | bytes 21762560 | tf_op jit(solution)/shard_map/dot_general | solution.py:109
  315.6 39.0 %reduce-scatter.2.cloned.1.call-done = f32[128,1024]{1,0:T(8,128)} async-done(((f32[128,8192]{1,0:T(8,128)}), f32[128,1024]{1,0:T(8,128)}) %reduce-scatter.2.cloned.1.call-update) | async-done | bytes 524304 | tf_op jit(solution)/shard_map/reduce_scatter | solution.py:112
  354.7 1.8 convert_element_type.22
  (77 shorter events, 21.9 us)
Async XLA Ops:
  6.5 189.7 %copy-start = (bf16[128,1024]{1,0:T(8,128)(2,1)S(1)}, bf16[128,1024]{1,0:T(8,128)(2,1)}, u32[]{:S(2)}) copy-start(bf16[128,1024]{1,0:T(8,128)(2,1)} %param.13) | copy-start | bytes 786436
  6.5 298.9 %copy-start.1 = (f32[1024]{0:T(1024)S(1)}, f32[1024]{0:T(1024)}, u32[]{:S(2)}) copy-start(f32[1024]{0:T(1024)} %param.20) | copy-start | bytes 12292
  6.5 148.7 %all-gather.7.cloned.1.call-start = ((), (), s32[]{:S(2)}) async-start(), calls=%async_computation.3 | async-start | bytes 17301504 | tf_op jit(solution)/shard_map/all_gather | solution.py:14
  12.6 292.8 %all-gather.5.cloned.1.call-start = ((), (), s32[]{:S(2)}) async-start(), calls=%async_computation.1 | async-start | bytes 17301504 | tf_op jit(solution)/shard_map/all_gather | solution.py:110
  13.4 341.3 %reduce-scatter.2.cloned.1.call-start = ((), (), s32[]{:S(2)}) async-start(), calls=%async_computation.2 | async-start | bytes 4718592 | tf_op jit(solution)/shard_map/reduce_scatter | solution.py:112
Sparse Core Ops, SparseCore 0:
  12.7 142.4 all-gather.6
  157.7 147.7 all-gather.4
  315.8 38.8 reduce-scatter.1
where the time goes:
time: 365 us; the launch traced here: 363 us
  waiting for transfers between devices  210 us (58%)
  blocking collectives  74.4 us (20%)
  other arithmetic  43.9 us (12%)
  matrix products  16.4 us (4%)
  between operations  13.9 us (4%)
    all_gather x1, waiting for transfers between devices, shards(): lax.all_gather(w_out, 'seq', axis=1, tiled=True)  109 us
    unnamed x1, blocking collectives  74.4 us
    all_gather x1, waiting for transfers between devices, prefix(): everything = jax.tree.map(lambda part: lax.all_gather(part, axis), array)  61.4 us
    reduce_scatter x1, waiting for transfers between devices, shards(): lax.psum_scatter(partial_out, 'grp', scatter_dimension=1, tiled=True)  39 us
    select_n x32, other arithmetic, turn(): return jax.tree.map(lambda a, b: jnp.where(reached, a, b), new, before)  37.7 us
    dot_general x1, matrix products, shards(): jnp.dot(normed, lax.all_gather(w_out, 'seq', axis=1, tiled=True), preferr...  10.2 us
  transfers between devices with their start and end apart: 3, of which 3 were waited for; matrix products, arithmetic and copies ran while one was open for 13% of the time, Pallas kernels for 0%

commit v1 on v0

--- a/solution.py
+++ b/solution.py
@@ -107,7 +107,11 @@
     y = y + skip_d[None, :, None] * xf
     normed = gated_norm_output(y, multiplier_channels, norm_gain, groups)
     partial_out = jnp.dot(
-        normed, lax.all_gather(w_out, "seq", axis=1, tiled=True), preferred_element_type=jnp.float32
+        normed,
+        jnp.concatenate(
+            lax.all_to_all(jnp.stack([w_out] * lax.axis_size("seq")), "seq", 0, 0), axis=1
+        ),
+        preferred_element_type=jnp.float32,
     )
     return lax.psum_scatter(partial_out, "grp", scatter_dimension=1, tiled=True).astype(
         jnp.bfloat16

time: 365 us -> 678 us (1.86)
  blocking collectives: 74.4 us -> 540 us
  waiting for transfers between devices: 210 us -> 37.4 us
  starting transfers between devices: 0.08 us -> 11.9 us
    unnamed x1, blocking collectives: 74.4 us -> 540 us
    all_gather x1 -> x0, waiting for transfers between devices: 109 us -> none  [shards(): lax.all_gather(w_out, 'seq', axis=1, tiled=True)]
    all_gather x1, waiting for transfers between devices: 61.4 us -> 0.02 us  [prefix(): everything = jax.tree.map(lambda part: lax.all_gather(part, axis), array)]
    all_to_all x0 -> x1, starting transfers between devices: none -> 11.9 us  [shards(): lax.all_to_all(jnp.stack([w_out] * lax.axis_size('seq')), 'seq', 0, 0)]
  transfers between devices with their start and end apart: 3 -> 3, of which waited for: 3 -> 1; matrix products, arithmetic and copies ran while one was open for 13% -> 7% of each run, Pallas kernels for 0% -> 0%
where the time goes in v1:
time: 678 us; the launch traced here: 676 us
  blocking collectives  540 us (80%)
  other arithmetic  43 us (6%)
  waiting for transfers between devices  37.4 us (6%)
  matrix products  18.2 us (3%)
  between operations  14.3 us (2%)
  starting transfers between devices  11.9 us (2%)
  local copies, waits for them, and re-layouts  10 us (1%)
    unnamed x1, blocking collectives  540 us
    select_n x32, other arithmetic, turn(): return jax.tree.map(lambda a, b: jnp.where(reached, a, b), new, before)  37.6 us
    reduce_scatter x1, waiting for transfers between devices, shards(): lax.psum_scatter(partial_out, 'grp', scatter_dimension=1, tiled=True)  37.4 us
  transfers between devices with their start and end apart: 3, of which 1 were waited for; matrix products, arithmetic and copies ran while one was open for 7% of the time, Pallas kernels for 0%

profile of v1, /device:TPU:8, one launch (start us, length us, event | category | flops | bytes accessed | tf_op | source)
XLA Modules:
  0.0 676.1 jit_solution(8699839942404803319)
XLA Ops:
  11.1 1.4 convolution_add_fusion
  12.6 1.2 copy.44
  13.8 6.0 stack.2
  19.8 11.9 %all-to-all-start = ((bf16[32,1024,256]{1,2,0:T(8,128)(2,1)}), bf16[32,1024,256]{1,2,0:T(8,128)(2,1)}, u32[]{:S(2)}, u32[]{:S(2)}) async-start(bf16[32,1024,256]{1,2,0:T(8,128)(2,1)} %stack.2), calls=%async_computation | async-start | bytes 33554432 | tf_op jit(solution)/shard_map/all_to_all | solution.py:112
  33.3 540.2 %all-reduce = f32[256]{0:T(256)S(1)} all-reduce(f32[256]{0:T(256)S(1)} %exponential_dynamic-update-slice_fusion), channel_id=2, replica_groups=mesh['seq'=32,'grp'=8] {'seq'}, use_global_device_ids=true, to_apply=%add | all-reduce | flops 256 | bytes 2048
  576.0 39.0 %while.9 = (s32[]{:T(128)}, f32[8,128,128]{2,1,0:T(8,128)S(1)}, s32[]{:T(128)}, f32[32,8]{1,0:T(8,128)S(1)}, f32[32,8,128,128]{3,2,1,0:T(8,128)}, /*index=5*/s32[]{:T(128)}, s32[]{:T(128)}) while((s32[]{:T(128)}, f32[8,128,128]{2,1,0:T(8,128)S(1)}, s32[]{:T(128)}, f32[32,8]{1,0:T(8,128)S(1)}, f32[32,8,128,128]{3,2,1,0:T(8,128)}, ...), condition=%wide.region_3.4_spmd.clone, body=%wide.region_2.3_spmd.clone.sunk | while | flops 524292 | bytes 1573073 | solution.py:26
  576.0 1.2 fusion.41
  577.3 1.2 fusion.41
  578.5 1.2 fusion.41
  579.7 1.2 fusion.41
  580.9 1.2 fusion.41
  582.1 1.2 fusion.41
  583.3 1.2 fusion.41
  584.6 1.2 fusion.41
  585.8 1.2 fusion.41
  587.0 1.2 fusion.41
  588.2 1.2 fusion.41
  589.4 1.2 fusion.41
  590.7 1.2 fusion.41
  591.9 1.2 fusion.41
  595.5 1.2 fusion.41
  596.7 1.2 fusion.41
  600.4 1.2 fusion.41
  601.6 1.2 fusion.41
  605.3 1.2 fusion.41
  608.9 1.2 fusion.41
  610.1 1.2 fusion.41
  613.8 1.2 fusion.41
  615.0 1.2 fusion.3
  616.7 13.4 %fusion.15 = f32[128,8192]{1,0:T(8,128)} fusion(bf16[1024,8192]{0,1:T(8,128)(2,1)} %bitcast.11, f32[1024]{0:T(1024)S(1)} %copy-done.3, f32[128]{0:T(128)S(1)} %add_rsqrt_fusion, f32[128,1024]{1,0:T(8,128)S(1)} %copy.43, bf16[128,1024]{1,0:T(8,128)(2,1)S(1)} %copy-done), kind=kOutput, calls=%fused_computation.27 | convolution fusion | flops 2148663296 | bytes 21762560 | tf_op jit(solution)/shard_map/dot_general | solution.py:109
  630.1 37.4 %reduce-scatter.2.cloned.1.call-done = f32[128,1024]{1,0:T(8,128)} async-done(((f32[128,8192]{1,0:T(8,128)}), f32[128,1024]{1,0:T(8,128)}) %reduce-scatter.2.cloned.1.call-update) | async-done | bytes 524304 | tf_op jit(solution)/shard_map/reduce_scatter | solution.py:116
  667.5 1.8 convert_element_type.24
  (86 shorter events, 20.4 us)
Async XLA Ops:
  6.5 569.5 %all-gather.4.cloned.1.call-start = ((), (), s32[]{:S(2)}) async-start(), calls=%async_computation.3 | async-start | bytes 17301504 | tf_op jit(solution)/shard_map/all_gather | solution.py:14
  19.8 12.0 %copy-start.5 = (u32[256]{0:T(256)S(1)}, u32[256]{0:T(256)}, u32[]{:S(2)}) copy-start(u32[256]{0:T(256)} %constant.71) | copy-start | bytes 3076
  19.8 553.8 %copy-start.2 = (bf16[128,128]{1,0:T(8,128)(2,1)S(1)}, bf16[128,128]{1,0:T(8,128)(2,1)}, u32[]{:S(2)}) copy-start(bf16[128,128]{1,0:T(8,128)(2,1)} %param.15) | copy-start | bytes 98308
  19.8 554.0 %copy-start.1 = (bf16[128,128]{1,0:T(8,128)(2,1)S(1)}, bf16[128,128]{1,0:T(8,128)(2,1)}, u32[]{:S(2)}) copy-start(bf16[128,128]{1,0:T(8,128)(2,1)} %param.14) | copy-start | bytes 98308
  19.8 595.2 %copy-start.4 = (f32[8]{0:T(128)S(1)}, f32[8]{0:T(128)}, u32[]{:S(2)}) copy-start(f32[8]{0:T(128)} %param.19) | copy-start | bytes 100
  19.8 596.6 %copy-start = (bf16[128,1024]{1,0:T(8,128)(2,1)S(1)}, bf16[128,1024]{1,0:T(8,128)(2,1)}, u32[]{:S(2)}) copy-start(bf16[128,1024]{1,0:T(8,128)(2,1)} %param.13) | copy-start | bytes 786436
  19.8 596.8 %copy-start.3 = (f32[1024]{0:T(1024)S(1)}, f32[1024]{0:T(1024)}, u32[]{:S(2)}) copy-start(f32[1024]{0:T(1024)} %param.20) | copy-start | bytes 12292
  19.8 596.8 %all-to-all-start = ((bf16[32,1024,256]{1,2,0:T(8,128)(2,1)}), bf16[32,1024,256]{1,2,0:T(8,128)(2,1)}, u32[]{:S(2)}, u32[]{:S(2)}) async-start(bf16[32,1024,256]{1,2,0:T(8,128)(2,1)} %stack.2), calls=%async_computation | async-start | bytes 33554432 | tf_op jit(solution)/shard_map/all_to_all | solution.py:112
  31.8 635.7 %reduce-scatter.2.cloned.1.call-start = ((), (), s32[]{:S(2)}) async-start(), calls=%async_computation.2 | async-start | bytes 4718592 | tf_op jit(solution)/shard_map/reduce_scatter | solution.py:116
Sparse Core Ops, SparseCore 0:
  12.7 432.0 all-gather.3
  630.2 37.2 reduce-scatter.1
